TPU v7x, 32 devices: a whole 2x2x4 slice. The times are simulated.
32 devices in a mesh: dp: 8 (over z, x), tensor: 4 (over y, core).
Axes of the slice: x: 2, y: 2, z: 4, core: 2. Of those that a mesh axis runs over, the one named last changes fastest.
Arguments:
- tokens: bfloat16 [16384, 768], P(('dp', 'tensor')), may hold values from -6 to 6
- stack: bfloat16 [4, 16384, 768], P(None, ('dp', 'tensor')), may hold values from -6 to 6
- cotangent: bfloat16 [16384, 768], P(('dp', 'tensor')), may hold values from -6 to 6
- starts: int32 [16, 2], P('dp'), may hold values from 0 to 768
- w_query: bfloat16 [768, 768], P('dp', 'tensor'), may hold values from -0.21875 to 0.21875
- w_key: bfloat16 [768, 768], P('dp', 'tensor'), may hold values from -0.21875 to 0.21875
- w_value: bfloat16 [768, 768], P('dp', 'tensor'), may hold values from -0.21875 to 0.21875
- w_output: bfloat16 [768, 768], P('tensor', 'dp'), may hold values from -0.875 to 0.875
- w_in: bfloat16 [768, 3072], P('dp', 'tensor'), may hold values from -0.21875 to 0.21875
- w_out: bfloat16 [3072, 768], P('tensor', 'dp'), may hold values from -0.109375 to 0.109375
- gain_one: float32 [768], replicated, may hold values from 0.1 to 1.9
- shift_one: float32 [768], replicated, may hold values from -3 to 3
- gain_two: float32 [768], replicated, may hold values from 0.1 to 1.9
- shift_two: float32 [768], replicated, may hold values from -3 to 3
- bias_in: float32 [3072], replicated, may hold values from -3 to 3
- bias_out: float32 [768], replicated, may hold values from -3 to 3
- depth_weights: float32 [5], replicated, may hold values from 0.3 to 1.2
Outputs:
- layer_out: bfloat16 [16384, 768], P(('dp', 'tensor'))
- grad_tokens: float32 [16384, 768], P(('dp', 'tensor'))
- grad_stack: float32 [4, 16384, 768], P(None, ('dp', 'tensor'))
- grad_w_query: float32 [768, 768], P('dp', 'tensor')
- grad_w_key: float32 [768, 768], P('dp', 'tensor')
- grad_w_value: float32 [768, 768], P('dp', 'tensor')
- grad_w_output: float32 [768, 768], P('tensor', 'dp')
- grad_w_in: float32 [768, 3072], P('dp', 'tensor')
- grad_w_out: float32 [3072, 768], P('tensor', 'dp')
- grad_gain_one: float32 [768], replicated
- grad_shift_one: float32 [768], replicated
- grad_gain_two: float32 [768], replicated
- grad_shift_two: float32 [768], replicated
- grad_bias_in: float32 [3072], replicated
- grad_bias_out: float32 [768], replicated
- grad_depth: float32 [5], replicated
All inputs are finite; a program needn't handle non-finite values.
Results may differ from a plain program's by a relative error of at most 0.012.
Values may be sent and summed in bfloat16 or wider, within the bound.
A program may use at most 128 MiB of HBM per device.

v0:
```python
import math
import jax
import jax.numpy as jnp
from jax import lax
from jax.sharding import PartitionSpec as P

HEAD_DIM = 64
PIECE = 256
EPSILON = 1e-05
NEGATIVE = -1e30


def layer_norm(values, gain, shift):
    centre = values - jnp.mean(values, axis=-1, keepdims=True)
    spread = jnp.mean(centre * centre, axis=-1, keepdims=True)
    return centre * lax.rsqrt(spread + EPSILON) * gain + shift


def tables(seq_length, head_size):
    half_dim = head_size // 2
    frequency = jnp.exp(
        -jnp.log(10000.0) * jnp.arange(half_dim, dtype=jnp.float32) * 2.0 / head_size
    )
    angles = jnp.arange(seq_length, dtype=jnp.float32)[:, None] * frequency[None, :]
    return (jnp.cos(angles), jnp.sin(angles))


def rotate(values, cosine_table, sine_table):
    half_dim = values.shape[-1] // 2
    front_half = values[..., :half_dim]
    back_half = values[..., half_dim:]
    cosines = cosine_table[:, None, :]
    sine_rows = sine_table[:, None, :]
    return jnp.concatenate(
        [
            front_half * cosines - back_half * sine_rows,
            back_half * cosines + front_half * sine_rows,
        ],
        axis=-1,
    )


def allowed_mask(starts, seq_length, piece_size):
    position = jnp.arange(seq_length, dtype=jnp.int32)
    inside = (position[None, None, :] >= starts[:, :, None]) & (
        position[None, None, :] < starts[:, :, None] + piece_size
    )
    jointly = jnp.any(inside[:, :, :, None] & inside[:, :, None, :], axis=1)
    return jointly | (position[None, :, None] >= position[None, None, :])


def gelu_tanh(values):
    return jax.nn.gelu(values, approximate=True)


def right_transposed(matrix, weight):
    return lax.dot_general(
        matrix, weight, (((1,), (1,)), ((), ())), preferred_element_type=jnp.float32
    )


def left_transposed(matrix, other):
    return lax.dot_general(
        matrix, other, (((0,), (0,)), ((), ())), preferred_element_type=jnp.float32
    )


def attend_forward(query, key_rows, value_rows, allowed, score_scale):

    def one_sequence(entries):
        query_seq, key_seq, value_seq, allowed_seq = entries
        scores = (
            jnp.einsum("qhd,khd->hqk", query_seq, key_seq, preferred_element_type=jnp.float32)
            * score_scale
        )
        scores = jnp.where(allowed_seq[None], scores, NEGATIVE)
        highest = jnp.max(scores, axis=-1, keepdims=True)
        powers = jnp.exp(scores - highest)
        row_total = jnp.sum(powers, axis=-1, keepdims=True)
        attention = (powers / row_total).astype(jnp.bfloat16)
        mixed_rows = jnp.einsum(
            "hqk,khd->qhd", attention, value_seq, preferred_element_type=jnp.float32
        )
        return (mixed_rows.astype(jnp.bfloat16), highest + jnp.log(row_total))

    return lax.map(one_sequence, (query, key_rows, value_rows, allowed))


def attend_backward(query, key_rows, value_rows, grad_mixed, log_totals, allowed, score_scale):

    def one_sequence(entries):
        query_seq, key_seq, value_seq, grad_seq, log_seq, allowed_seq = entries
        scores = (
            jnp.einsum("qhd,khd->hqk", query_seq, key_seq, preferred_element_type=jnp.float32)
            * score_scale
        )
        scores = jnp.where(allowed_seq[None], scores, NEGATIVE)
        attention = jnp.exp(scores - log_seq)
        grad_value = jnp.einsum(
            "hqk,qhd->khd",
            attention.astype(jnp.bfloat16),
            grad_seq,
            preferred_element_type=jnp.float32,
        )
        grad_attention = jnp.einsum(
            "qhd,khd->hqk", grad_seq, value_seq, preferred_element_type=jnp.float32
        )
        row_delta = jnp.sum(attention * grad_attention, axis=-1, keepdims=True)
        grad_scores = (attention * (grad_attention - row_delta)).astype(jnp.bfloat16)
        grad_query = (
            jnp.einsum("hqk,khd->qhd", grad_scores, key_seq, preferred_element_type=jnp.float32)
            * score_scale
        )
        grad_key = (
            jnp.einsum("hqk,qhd->khd", grad_scores, query_seq, preferred_element_type=jnp.float32)
            * score_scale
        )
        return (grad_query, grad_key, grad_value.astype(jnp.bfloat16))

    return lax.map(one_sequence, (query, key_rows, value_rows, grad_mixed, log_totals, allowed))


def per_device(
    tokens,
    stack,
    cotangent,
    starts,
    w_query,
    w_key,
    w_value,
    w_output,
    w_in,
    w_out,
    gain_one,
    shift_one,
    gain_two,
    shift_two,
    bias_in,
    bias_out,
    depth_weights,
):
    rows_here = tokens.shape[0]
    features = tokens.shape[1]
    groups = lax.axis_size("tensor")
    position = lax.axis_index("tensor")
    seq_count = starts.shape[0]
    seq_length = rows_here * groups // seq_count
    score_scale = 1.0 / math.sqrt(HEAD_DIM)
    local_heads = w_query.shape[1] // HEAD_DIM
    hidden = w_in.shape[1]
    cosine_table, sine_table = tables(seq_length, HEAD_DIM)
    allowed = allowed_mask(starts, seq_length, PIECE)

    def to_heads(matrix):
        return matrix.reshape(seq_count, seq_length, local_heads, HEAD_DIM)

    def from_heads(blocks):
        return blocks.reshape(seq_count * seq_length, local_heads * HEAD_DIM)

    def share_rows(local_rows):
        return lax.all_gather(local_rows, "tensor", axis=0, tiled=True)

    def share_grad(local_rows):
        return lax.all_gather(local_rows, "tensor", axis=0, tiled=True)

    def merge_rows(source, weight):
        return lax.psum_scatter(
            jnp.dot(source, weight, preferred_element_type=jnp.float32),
            "tensor",
            scatter_dimension=0,
            tiled=True,
        )

    def return_rows(pairs):
        running = jnp.zeros((lax.axis_size("tensor") * rows_here, features), jnp.float32)
        for source, weight in pairs:
            running = running + right_transposed(source, weight)
        return lax.psum_scatter(running, "tensor", scatter_dimension=0, tiled=True)

    query_w, key_w, value_w, output_w = (
        lax.all_gather(w_query, "dp", axis=0, tiled=True),
        lax.all_gather(w_key, "dp", axis=0, tiled=True),
        lax.all_gather(w_value, "dp", axis=0, tiled=True),
        lax.all_gather(w_output, "dp", axis=1, tiled=True),
    )
    inner_w, outer_w = (
        lax.all_gather(w_in, "dp", axis=0, tiled=True),
        lax.all_gather(w_out, "dp", axis=1, tiled=True),
    )
    token_rows = tokens.astype(jnp.float32)
    normed_one = layer_norm(token_rows, gain_one, shift_one).astype(jnp.bfloat16)
    normed_all = share_rows(normed_one)
    query = rotate(
        to_heads(jnp.dot(normed_all, query_w, preferred_element_type=jnp.float32)),
        cosine_table,
        sine_table,
    ).astype(jnp.bfloat16)
    key_rows = rotate(
        to_heads(jnp.dot(normed_all, key_w, preferred_element_type=jnp.float32)),
        cosine_table,
        sine_table,
    ).astype(jnp.bfloat16)
    value_rows = to_heads(jnp.dot(normed_all, value_w, preferred_element_type=jnp.float32)).astype(
        jnp.bfloat16
    )
    mixed_heads, log_totals = attend_forward(query, key_rows, value_rows, allowed, score_scale)
    mixed_flat = from_heads(mixed_heads)
    middle = token_rows + merge_rows(mixed_flat, output_w)
    normed_two = layer_norm(middle, gain_two, shift_two).astype(jnp.bfloat16)
    second_all = share_rows(normed_two)
    bias_slice = lax.dynamic_slice_in_dim(bias_in, position * hidden, hidden)
    pre_act = jnp.dot(second_all, inner_w, preferred_element_type=jnp.float32) + bias_slice
    activated = gelu_tanh(pre_act).astype(jnp.bfloat16)
    block_out = middle + merge_rows(activated, outer_w) + bias_out
    averaged = depth_weights[4] * block_out
    for layer_index in range(4):
        averaged = averaged + depth_weights[layer_index] * stack[layer_index].astype(jnp.float32)
    layer_out = averaged.astype(jnp.bfloat16)
    grad_rows = cotangent.astype(jnp.float32)
    grad_stack = jnp.stack([depth_weights[layer_index] * grad_rows for layer_index in range(4)])
    depth_terms = jnp.stack(
        [jnp.sum(stack[layer_index].astype(jnp.float32) * grad_rows) for layer_index in range(4)]
        + [jnp.sum(block_out * grad_rows)]
    )
    grad_block = depth_weights[4] * grad_rows
    grad_bias_out = jnp.sum(grad_block, axis=0)
    grad_sent = share_grad(grad_block.astype(jnp.bfloat16))
    grad_outer = left_transposed(activated, grad_sent)
    grad_act = right_transposed(grad_sent, outer_w)
    grad_pre = jax.vjp(gelu_tanh, pre_act)[1](grad_act)[0].astype(jnp.bfloat16)
    grad_bias_slice = jnp.sum(grad_pre.astype(jnp.float32), axis=0)
    bias_full = lax.dynamic_update_slice_in_dim(
        jnp.zeros((bias_in.shape[0],), jnp.float32), grad_bias_slice, position * hidden, 0
    )
    grad_inner = left_transposed(second_all, grad_pre)
    grad_norm_two = return_rows(((grad_pre, inner_w),))
    layer_two = jax.vjp(layer_norm, middle, gain_two, shift_two)[1](grad_norm_two)
    grad_middle = grad_block + layer_two[0]
    grad_attn_sent = share_grad(grad_middle.astype(jnp.bfloat16))
    grad_output_w = left_transposed(mixed_flat, grad_attn_sent)
    grad_mixed = right_transposed(grad_attn_sent, output_w).astype(jnp.bfloat16)
    grad_query, grad_key, grad_value = attend_backward(
        query, key_rows, value_rows, to_heads(grad_mixed), log_totals, allowed, score_scale
    )
    grad_query = from_heads(rotate(grad_query, cosine_table, -sine_table)).astype(jnp.bfloat16)
    grad_key = from_heads(rotate(grad_key, cosine_table, -sine_table)).astype(jnp.bfloat16)
    grad_value = from_heads(grad_value)
    grad_query_w = left_transposed(normed_all, grad_query)
    grad_key_w = left_transposed(normed_all, grad_key)
    grad_value_w = left_transposed(normed_all, grad_value)
    grad_norm_one = return_rows(((grad_query, query_w), (grad_key, key_w), (grad_value, value_w)))
    layer_one = jax.vjp(layer_norm, token_rows, gain_one, shift_one)[1](grad_norm_one)
    grad_tokens = grad_middle + layer_one[0]
    grad_w_query, grad_w_key, grad_w_value, grad_w_output, grad_w_in, grad_w_out = (
        lax.psum_scatter(grad_query_w, "dp", scatter_dimension=0, tiled=True),
        lax.psum_scatter(grad_key_w, "dp", scatter_dimension=0, tiled=True),
        lax.psum_scatter(grad_value_w, "dp", scatter_dimension=0, tiled=True),
        lax.psum_scatter(grad_output_w, "dp", scatter_dimension=1, tiled=True),
        lax.psum_scatter(grad_inner, "dp", scatter_dimension=0, tiled=True),
        lax.psum_scatter(grad_outer, "dp", scatter_dimension=1, tiled=True),
    )
    summed = lax.psum(
        (
            layer_one[1],
            layer_one[2],
            layer_two[1],
            layer_two[2],
            bias_full,
            grad_bias_out,
            depth_terms,
        ),
        ("dp", "tensor"),
    )
    return (
        layer_out,
        grad_tokens,
        grad_stack,
        grad_w_query,
        grad_w_key,
        grad_w_value,
        grad_w_output,
        grad_w_in,
        grad_w_out,
        summed[0],
        summed[1],
        summed[2],
        summed[3],
        summed[4],
        summed[5],
        summed[6],
    )


def solution(mesh):
    in_specs = (
        P(("dp", "tensor"), None),
        P(None, ("dp", "tensor"), None),
        P(("dp", "tensor"), None),
        P("dp", None),
        P("dp", "tensor"),
        P("dp", "tensor"),
        P("dp", "tensor"),
        P("tensor", "dp"),
        P("dp", "tensor"),
        P("tensor", "dp"),
        P(),
        P(),
        P(),
        P(),
        P(),
        P(),
        P(),
    )
    out_specs = (
        P(("dp", "tensor"), None),
        P(("dp", "tensor"), None),
        P(None, ("dp", "tensor"), None),
        P("dp", "tensor"),
        P("dp", "tensor"),
        P("dp", "tensor"),
        P("tensor", "dp"),
        P("dp", "tensor"),
        P("tensor", "dp"),
        P(),
        P(),
        P(),
        P(),
        P(),
        P(),
        P(),
    )
    return jax.shard_map(
        per_device, mesh=mesh, in_specs=in_specs, out_specs=out_specs, check_vma=False
    )
```

profile of v0, /device:TPU:0, one launch (start us, length us, event | category | flops | bytes accessed | tf_op | source)
XLA Modules:
  0.0 1099.3 jit_solution(18201807398381428645)
XLA Ops:
  14.7 2.9 and_reduce_fusion
  18.9 4.5 copy.84
  23.3 34.9 %all_gather.34 = bf16[192,768]{0,1:T(8,128)(2,1)} all-gather(bf16[192,96]{0,1:T(8,128)(2,1)S(1)} %copy.86), channel_id=1, replica_groups=mesh['dp'=8,'tensor'=4] {'dp'}, dimensions={1}, use_global_device_ids=true | all-gather | bytes 331776 | tf_op jit(solution)/shard_map/all_gather | solution.py:184
  58.3 33.1 %all_gather.32 = bf16[768,192]{1,0:T(8,128)(2,1)} all-gather(bf16[96,192]{1,0:T(8,128)(2,1)S(1)} %copy-done.46), channel_id=1, replica_groups=mesh['dp'=8,'tensor'=4] {'dp'}, dimensions={0}, use_global_device_ids=true | all-gather | bytes 331776 | tf_op jit(solution)/shard_map/all_gather | solution.py:181
  91.4 31.1 %all_gather.33 = bf16[768,192]{1,0:T(8,128)(2,1)S(1)} all-gather(bf16[96,192]{1,0:T(8,128)(2,1)S(1)} %copy-done.47), channel_id=1, replica_groups=mesh['dp'=8,'tensor'=4] {'dp'}, dimensions={0}, use_global_device_ids=true | all-gather | bytes 331776 | tf_op jit(solution)/shard_map/all_gather | solution.py:182
  122.5 33.5 %all_gather.31 = bf16[768,192]{1,0:T(8,128)(2,1)} all-gather(bf16[96,192]{1,0:T(8,128)(2,1)S(1)} %copy-done.48), channel_id=1, replica_groups=mesh['dp'=8,'tensor'=4] {'dp'}, dimensions={0}, use_global_device_ids=true | all-gather | bytes 331776 | tf_op jit(solution)/shard_map/all_gather | solution.py:183
  157.3 4.2 convolution_convert_fusion.1
  161.5 3.2 convert_element_type.101
  164.7 2.2 copy.83
  166.9 2.3 fusion.107
  169.3 3.4 reshape.244
  172.7 3.2 fusion.103
  175.9 2.3 fusion.106
  178.2 2.6 reshape.243
  185.7 29.1 %while.26 = (s32[]{:T(128)}, bf16[2,1024,3,64]{1,3,2,0:T(8,128)(2,1)}, f32[2,3,1024,1]{2,1,3,0:T(4,128)}, bf16[2,1024,3,64]{1,3,2,0:T(8,128)(2,1)}, pred[2,1024,...) while((s32[]{:T(128)}, ...), condition=%wide.region_6.7_spmd, body=%wide.region_3.6_spmd.sunk | while | flops 843248640 | bytes 55154872 | solution.py:86
  187.5 2.6 fusion.174
  190.1 3.9 fusion.175
  194.0 5.7 fusion.176
  202.0 2.6 fusion.174
  204.6 3.9 fusion.175
  208.5 5.7 fusion.176
  214.8 2.0 copy.85
  217.9 3.8 fusion.108
  222.3 59.0 %reduce-scatter.13.cloned.1.call-done = f32[512,768]{1,0:T(8,128)} async-done(((f32[2048,768]{1,0:T(8,128)}), f32[512,768]{1,0:T(8,128)}) %reduce-scatter.13.cloned.1.call-update) | async-done | bytes 1572880 | tf_op jit(solution)/shard_map/reduce_scatter | solution.py:167
  288.3 24.7 %all-gather.9.cloned.1.call-done = bf16[2048,768]{1,0:T(8,128)(2,1)} async-done(((bf16[512,768]{1,0:T(8,128)(2,1)}), bf16[2048,768]{1,0:T(8,128)(2,1)}) %all-gather.9.cloned.1.call-update) | async-done | bytes 3145744 | tf_op jit(solution)/shard_map/all_gather | solution.py:161
  313.0 7.5 fusion.109
  320.6 36.3 %all-gather.13.cloned.1.call-done = bf16[768,768]{0,1:T(8,128)(2,1)} async-done(((bf16[768,96]{0,1:T(8,128)(2,1)}), bf16[768,768]{0,1:T(8,128)(2,1)}) %all-gather.13.cloned.1.call-update) | async-done | bytes 1179664 | tf_op jit(solution)/shard_map/all_gather | solution.py:188
  356.9 29.1 %all-gather.15.cloned.1.call-done = bf16[2048,768]{1,0:T(8,128)(2,1)} async-done(((bf16[512,768]{1,0:T(8,128)(2,1)}), bf16[2048,768]{1,0:T(8,128)(2,1)}) %all-gather.15.cloned.1.call-update) | async-done | bytes 3145744 | tf_op jit(solution)/shard_map/all_gather | solution.py:164
  386.0 11.1 %convert_reduce_fusion = (f32[768]{0:T(1024)}, bf16[2048,768]{1,0:T(8,128)(2,1)S(1)}, bf16[2048,768]{1,0:T(8,128)(2,1)}) fusion(f32[2048,768]{1,0:T(8,128)} %fusion.109, f32[768]{0:T(1024)S(1)} %dynamic_slice.36, bf16[2048,768]{1,0:T(8,128)(2,1)} %all-gather.15.cloned.1.call-done, bf16[768,768]{0,1:T(8,128)(2,1)} %all-gather.13.cloned.1.call-done), kind=kOutput, calls=%fused_computation.73 | convolution fusion | flops 2455239936 | bytes 16914432 | tf_op jit(solution)/shard_map/dot_general | solution.py:57
  398.8 4.5 fusion.111
  403.4 8.0 fusion.110
  411.5 50.2 %reduce-scatter.17.cloned.1.call-done = f32[512,768]{1,0:T(8,128)} async-done(((f32[2048,768]{1,0:T(8,128)}), f32[512,768]{1,0:T(8,128)}) %reduce-scatter.17.cloned.1.call-update) | async-done | bytes 1572880 | tf_op jit(solution)/shard_map/reduce_scatter | solution.py:178
  461.7 60.8 %reduce-scatter.15.cloned.1.call-done = f32[512,768]{1,0:T(8,128)} async-done(((f32[2048,768]{1,0:T(8,128)}), f32[512,768]{1,0:T(8,128)}) %reduce-scatter.15.cloned.1.call-update) | async-done | bytes 1572880 | tf_op jit(solution)/shard_map/reduce_scatter | solution.py:167
  522.5 8.1 multiply_reduce_fusion.1
  534.4 28.6 %all-gather.17.cloned.1.call-done = bf16[2048,768]{1,0:T(8,128)(2,1)} async-done(((bf16[512,768]{1,0:T(8,128)(2,1)}), bf16[2048,768]{1,0:T(8,128)(2,1)}) %all-gather.17.cloned.1.call-update) | async-done | bytes 3145744 | tf_op jit(solution)/shard_map/all_gather | solution.py:164
  563.0 3.1 convolution_convert_fusion
  569.9 51.6 %while.27 = (s32[]{:T(128)}, f32[2,1024,3,64]{1,3,2,0:T(8,128)}, f32[2,1024,3,64]{1,3,2,0:T(8,128)}, bf16[2,1024,3,64]{1,3,2,0:T(8,128)(2,1)}, bf16[2,1024,3,64]...) while((s32[]{:T(128)}, f32[2,1024,3,64]{1,3,2,0:T(8,128)}, ...), condition=%wide.region_16.17_spmd, body=%wide.region_14.16_spmd.sunk | while | flops 2061038592 | bytes 135890256 | solution.py:120
  573.5 3.7 fusion.188
  577.2 7.1 multiply_reduce_fusion.5
  584.4 7.1 multiply_convert_fusion.3
  591.5 2.0 fusion.187
  599.1 3.7 fusion.188
  602.8 7.1 multiply_reduce_fusion.5
  610.0 7.1 multiply_convert_fusion.3
  617.1 2.0 fusion.187
  621.5 4.5 convolution_bitcast_fusion
  633.5 3.8 add_add_fusion
  639.3 6.0 fusion.117
  645.6 7.1 fusion.118
  652.7 3.0 fusion.116
  655.9 3.1 fusion.115
  659.4 4.1 fusion.114
  663.5 25.3 %reduce-scatter.31.cloned.1.call-done = f32[96,192]{1,0:T(8,128)} async-done(((f32[768,192]{1,0:T(8,128)}), f32[96,192]{1,0:T(8,128)}) %reduce-scatter.31.cloned.1.call-update) | async-done | bytes 73744
  690.4 58.6 %reduce-scatter.19.cloned.1.call-done = f32[512,768]{1,0:T(8,128)} async-done(((f32[2048,768]{1,0:T(8,128)}), f32[512,768]{1,0:T(8,128)}) %reduce-scatter.19.cloned.1.call-update) | async-done | bytes 1572880 | tf_op jit(solution)/shard_map/reduce_scatter | solution.py:178
  749.0 2.0 fusion.99
  751.9 8.8 fusion.90
  760.7 3.4 stack.43
  764.1 40.7 %all-reduce = (f32[768]{0:T(1024)}, f32[768]{0:T(1024)}, f32[768]{0:T(1024)}, f32[768]{0:T(1024)}, f32[3072]{0:T(1024)}, /*index=5*/f32[768]{0:T(1024)}, f32[5]{0:T(128)}) all-reduce(f32[768]{0:T(1024)S(1)} %get-tuple-element.187, f32[768]{0:T(1024)S(1)} %get-tuple-element.191, ...), channel_id=1, replica_groups=mesh['dp'=8,'tensor'=4] {'dp','tensor'}, use_global_device_ids=true, to_apply=%region_27.28 | all-reduce | flops 6917 | bytes 55336 | tf_op jit(solution)/shard_map/psum | solution.py:262
  804.8 4.6 pad_maximum_fusion
  809.4 13.0 %reduce-scatter.27.cloned.1.call-done = f32[96,768]{1,0:T(8,128)} async-done(((f32[768,768]{1,0:T(8,128)}), f32[96,768]{1,0:T(8,128)}) %reduce-scatter.27.cloned.1.call-update) | async-done | bytes 294928 | tf_op jit(solution)/shard_map/reduce_scatter | solution.py:259
  822.5 72.5 %reduce-scatter.29.cloned.1.call-done = f32[768,96]{0,1:T(8,128)} async-done(((f32[768,768]{0,1:T(8,128)}), f32[768,96]{0,1:T(8,128)}) %reduce-scatter.29.cloned.1.call-update) | async-done | bytes 294928 | tf_op jit(solution)/shard_map/reduce_scatter | solution.py:260
  894.9 65.7 %reduce-scatter.25.cloned.1.call-done = f32[96,192]{1,0:T(8,128)} async-done(((f32[768,192]{1,0:T(8,128)}), f32[96,192]{1,0:T(8,128)}) %reduce-scatter.25.cloned.1.call-update) | async-done | bytes 73744 | tf_op jit(solution)/shard_map/reduce_scatter | solution.py:257
  960.7 65.4 %reduce-scatter.23.cloned.1.call-done = f32[96,192]{1,0:T(8,128)} async-done(((f32[768,192]{1,0:T(8,128)}), f32[96,192]{1,0:T(8,128)}) %reduce-scatter.23.cloned.1.call-update) | async-done | bytes 73744 | tf_op jit(solution)/shard_map/reduce_scatter | solution.py:256
  1026.1 65.6 %reduce-scatter.21.cloned.1.call-done = f32[96,192]{1,0:T(8,128)} async-done(((f32[768,192]{1,0:T(8,128)}), f32[96,192]{1,0:T(8,128)}) %reduce-scatter.21.cloned.1.call-update) | async-done | bytes 73744 | tf_op jit(solution)/shard_map/reduce_scatter | solution.py:255
  (250 shorter events, 59.9 us)
Async XLA Ops:
  8.0 4.1 copy-start.1
  8.0 6.2 copy-start.49
  8.0 149.3 %all-gather.7.cloned.1.call-start = ((), (), s32[]{:S(2)}) async-start(), calls=%async_computation.10 | async-start | bytes 3932160 | tf_op jit(solution)/shard_map/all_gather | solution.py:161
  9.5 2.1 copy-start.43
  9.5 5.1 copy-start.62
  14.1 267.2 %reduce-scatter.13.cloned.1.call-start = ((), (), s32[]{:S(2)}) async-start(), calls=%async_computation.11 | async-start | bytes 7864320 | tf_op jit(solution)/shard_map/reduce_scatter | solution.py:167
  18.8 39.5 %copy-start.46 = (bf16[96,192]{1,0:T(8,128)(2,1)S(1)}, bf16[96,192]{1,0:T(8,128)(2,1)}, u32[]{:S(2)}) copy-start(bf16[96,192]{1,0:T(8,128)(2,1)} %param.25) | copy-start | bytes 110596
  18.8 72.5 %copy-start.47 = (bf16[96,192]{1,0:T(8,128)(2,1)S(1)}, bf16[96,192]{1,0:T(8,128)(2,1)}, u32[]{:S(2)}) copy-start(bf16[96,192]{1,0:T(8,128)(2,1)} %param.26) | copy-start | bytes 110596
  18.8 103.6 %copy-start.48 = (bf16[96,192]{1,0:T(8,128)(2,1)S(1)}, bf16[96,192]{1,0:T(8,128)(2,1)}, u32[]{:S(2)}) copy-start(bf16[96,192]{1,0:T(8,128)(2,1)} %param.27) | copy-start | bytes 110596
  122.5 44.4 %copy-start.20 = (bf16[768,192]{1,0:T(8,128)(2,1)}, bf16[768,192]{1,0:T(8,128)(2,1)S(1)}, u32[]{:S(2)}) copy-start(bf16[768,192]{1,0:T(8,128)(2,1)S(1)} %all_gather.33) | copy-start | bytes 884740
  157.3 9.6 copy-start.8
  172.7 3.2 copy-start.22
  187.5 2.6 copy-start
  202.0 2.6 copy-start
  214.8 3.1 copy-start.24
  221.7 59.7 %copy-start.2 = (bf16[512,768]{1,0:T(8,128)(2,1)S(1)}, bf16[512,768]{1,0:T(8,128)(2,1)}, u32[]{:S(2)}) copy-start(bf16[512,768]{1,0:T(8,128)(2,1)} %param.21) | copy-start | bytes 2359300
  221.7 66.6 %all-gather.11.cloned.1.call-start = ((), (), s32[]{:S(2)}) async-start(), calls=%async_computation.13 | async-start | bytes 1327104 | tf_op jit(solution)/shard_map/all_gather | solution.py:187
  222.3 61.0 %copy-start.50 = (f32[768]{0:T(1024)S(1)}, f32[768]{0:T(1024)}, u32[]{:S(2)}) copy-start(f32[768]{0:T(1024)} %param.33) | copy-start | bytes 9220
  222.3 61.0 %copy-start.60 = (f32[768]{0:T(1024)S(1)}, f32[768]{0:T(1024)}, u32[]{:S(2)}) copy-start(f32[768]{0:T(1024)} %param.34) | copy-start | bytes 9220
  222.3 90.8 %all-gather.9.cloned.1.call-start = ((), (), s32[]{:S(2)}) async-start(), calls=%async_computation.12 | async-start | bytes 3932160 | tf_op jit(solution)/shard_map/all_gather | solution.py:161
  283.0 2.2 copy-start.59
  283.0 2.8 copy-start.13
  284.5 72.4 %all-gather.13.cloned.1.call-start = ((), (), s32[]{:S(2)}) async-start(), calls=%async_computation.14 | async-start | bytes 1327104 | tf_op jit(solution)/shard_map/all_gather | solution.py:188
  285.1 100.9 %all-gather.15.cloned.1.call-start = ((), (), s32[]{:S(2)}) async-start(), calls=%async_computation.16 | async-start | bytes 3932160 | tf_op jit(solution)/shard_map/all_gather | solution.py:164
  287.5 174.2 %reduce-scatter.17.cloned.1.call-start = ((), (), s32[]{:S(2)}) async-start(), calls=%async_computation.17 | async-start | bytes 7864320 | tf_op jit(solution)/shard_map/reduce_scatter | solution.py:178
  386.0 12.8 %copy-start.65 = (bf16[768,768]{1,0:T(8,128)(2,1)S(1)}, bf16[768,768]{1,0:T(8,128)(2,1)}, u32[]{:S(2)}) copy-start(bf16[768,768]{1,0:T(8,128)(2,1)} %all-gather.11.cloned.1.call-done) | copy-start | bytes 3538948
  403.3 119.2 %reduce-scatter.15.cloned.1.call-start = ((), (), s32[]{:S(2)}) async-start(), calls=%async_computation.15 | async-start | bytes 7864320 | tf_op jit(solution)/shard_map/reduce_scatter | solution.py:167
  411.4 111.1 %copy-start.61 = (f32[768]{0:T(1024)S(1)}, f32[768]{0:T(1024)}, u32[]{:S(2)}) copy-start(f32[768]{0:T(1024)} %param.36) | copy-start | bytes 9220
  411.4 151.5 %all-gather.17.cloned.1.call-start = ((), (), s32[]{:S(2)}) async-start(), calls=%async_computation.18 | async-start | bytes 3932160 | tf_op jit(solution)/shard_map/all_gather | solution.py:164
  522.5 8.1 copy-start.16
  534.3 154.5 %reduce-scatter.31.cloned.1.call-start = ((), (), s32[]{:S(2)}) async-start(), calls=%async_computation.25 | async-start | bytes 884736
  566.1 3.8 copy-start.5
  566.1 3.8 copy-start.7
  566.1 3.8 copy-start.15
  567.6 2.3 copy-start.42
  577.2 7.1 copy-start.30
  584.4 7.1 copy-start.32
  591.5 2.1 copy-start.35
  602.8 7.1 copy-start.30
  610.0 7.1 copy-start.32
  621.5 4.8 copy-start.34
  621.5 4.8 copy-start.37
  621.5 4.8 copy-start.39
  621.5 4.8 copy-start.40
  626.0 122.9 %reduce-scatter.19.cloned.1.call-start = ((), (), s32[]{:S(2)}) async-start(), calls=%async_computation.19 | async-start | bytes 7864320 | tf_op jit(solution)/shard_map/reduce_scatter | solution.py:178
  631.2 2.1 copy-start.26
  637.4 185.1 %reduce-scatter.27.cloned.1.call-start = ((), (), s32[]{:S(2)}) async-start(), calls=%async_computation.23 | async-start | bytes 2654208 | tf_op jit(solution)/shard_map/reduce_scatter | solution.py:259
  645.3 249.7 %reduce-scatter.29.cloned.1.call-start = ((), (), s32[]{:S(2)}) async-start(), calls=%async_computation.24 | async-start | bytes 2654208 | tf_op jit(solution)/shard_map/reduce_scatter | solution.py:260
  645.6 7.2 copy-start.9
  652.7 308.0 %reduce-scatter.25.cloned.1.call-start = ((), (), s32[]{:S(2)}) async-start(), calls=%async_computation.22 | async-start | bytes 884736 | tf_op jit(solution)/shard_map/reduce_scatter | solution.py:257
  655.8 3.2 copy-start.63
  655.8 370.3 %reduce-scatter.23.cloned.1.call-start = ((), (), s32[]{:S(2)}) async-start(), calls=%async_computation.21 | async-start | bytes 884736 | tf_op jit(solution)/shard_map/reduce_scatter | solution.py:256
  659.0 432.8 %reduce-scatter.21.cloned.1.call-start = ((), (), s32[]{:S(2)}) async-start(), calls=%async_computation.20 | async-start | bytes 884736 | tf_op jit(solution)/shard_map/reduce_scatter | solution.py:255
  659.3 89.6 %copy-start.3 = (bf16[512,768]{1,0:T(8,128)(2,1)S(1)}, bf16[512,768]{1,0:T(8,128)(2,1)}, u32[]{:S(2)}) copy-start(bf16[512,768]{1,0:T(8,128)(2,1)} %param.21) | copy-start | bytes 2359300
  659.3 89.6 %copy-start.44 = (f32[512]{0:T(512)S(1)}, f32[512]{0:T(512)}, u32[]{:S(2)}) copy-start(f32[512]{0:T(512)} %copy-done.43) | copy-start | bytes 6148
  659.3 89.6 %copy-start.45 = (f32[768]{0:T(1024)S(1)}, f32[768]{0:T(1024)}, u32[]{:S(2)}) copy-start(f32[768]{0:T(1024)} %param.31) | copy-start | bytes 9220
  663.4 87.6 %copy-start.56 = (f32[512]{0:T(512)S(1)}, f32[512]{0:T(512)}, u32[]{:S(2)}) copy-start(f32[512]{0:T(512)} %copy-done.55) | copy-start | bytes 6148
  663.4 87.6 %copy-start.52 = (f32[512]{0:T(512)S(1)}, f32[512]{0:T(512)}, u32[]{:S(2)}) copy-start(f32[512]{0:T(512)} %copy-done.51) | copy-start | bytes 6148
  690.4 61.5 %copy-start.14 = (bf16[512,768]{1,0:T(8,128)(2,1)S(1)}, bf16[512,768]{1,0:T(8,128)(2,1)}, u32[]{:S(2)}) copy-start(bf16[512,768]{1,0:T(8,128)(2,1)} %param.23) | copy-start | bytes 2359300
  690.4 61.5 %copy-start.54 = (f32[512]{0:T(512)S(1)}, f32[512]{0:T(512)}, u32[]{:S(2)}) copy-start(f32[512]{0:T(512)} %copy-done.53) | copy-start | bytes 6148
  749.0 2.1 copy-start.10
  749.0 2.9 copy-start.12
  751.9 12.2 %copy-start.57 = (f32[768]{0:T(1024)S(1)}, f32[768]{0:T(1024)}, u32[]{:S(2)}) copy-start(f32[768]{0:T(1024)} %get-tuple-element.185) | copy-start | bytes 9220
  751.9 12.2 %copy-start.58 = (f32[768]{0:T(1024)S(1)}, f32[768]{0:T(1024)}, u32[]{:S(2)}) copy-start(f32[768]{0:T(1024)} %get-tuple-element.190) | copy-start | bytes 9220
  (28 other events, 37.0 us)
Sparse Core Ops, SparseCore 0:
  14.2 31.2 all-gather.6
  221.8 59.4 reduce-scatter.12
  534.4 28.5 all-gather.16
Sparse Core Ops, SparseCore 1:
  224.3 42.6 all-gather.10
  284.6 28.4 all-gather.8
  315.3 41.5 all-gather.12
  359.1 26.8 all-gather.14
  403.4 58.2 reduce-scatter.16
  464.2 58.2 reduce-scatter.14
  626.1 62.6 reduce-scatter.30
  691.7 57.2 reduce-scatter.18
  753.3 69.1 reduce-scatter.26
  826.9 67.9 reduce-scatter.28
  899.0 61.6 reduce-scatter.24
  964.6 61.5 reduce-scatter.22
  1030.2 61.5 reduce-scatter.20
where the time goes:
time: 1110 us; the launch traced here: 1100 us
  waiting for transfers between devices  656 us (59%)
  blocking collectives  173 us (16%)
  matrix products  129 us (12%)
  other arithmetic  68.3 us (6%)
  local copies, waits for them, and re-layouts  53.7 us (5%)
  between operations  16.6 us (1%)
    reduce_scatter x2, waiting for transfers between devices, merge_rows(): lax.psum_scatter(jnp.dot(source, weight, preferred_element_type=jnp.float...  120 us
    reduce_scatter x2, waiting for transfers between devices, return_rows(): return lax.psum_scatter(running, 'tensor', scatter_dimension=0, tiled=True)  109 us
    reduce_scatter x1, waiting for transfers between devices, per_device(): lax.psum_scatter(grad_outer, 'dp', scatter_dimension=1, tiled=True)  72.5 us
    reduce_scatter x1, waiting for transfers between devices, per_device(): lax.psum_scatter(grad_value_w, 'dp', scatter_dimension=0, tiled=True)  65.7 us
    reduce_scatter x1, waiting for transfers between devices, per_device(): lax.psum_scatter(grad_query_w, 'dp', scatter_dimension=0, tiled=True)  65.6 us
    reduce_scatter x1, waiting for transfers between devices, per_device(): lax.psum_scatter(grad_key_w, 'dp', scatter_dimension=0, tiled=True)  65.4 us
    all_gather x2, waiting for transfers between devices, share_grad(): return lax.all_gather(local_rows, 'tensor', axis=0, tiled=True)  57.7 us
    psum x1, blocking collectives, per_device(): lax.psum((layer_one[1], layer_one[2], layer_two[1], layer_two[2], bias_fu...  40.7 us
  transfers between devices with their start and end apart: 16, of which 14 were waited for; matrix products, arithmetic and copies ran while one was open for 8% of the time, Pallas kernels for 0%

commit v1 on v0

--- a/solution.py
+++ b/solution.py
@@ -8,6 +8,24 @@
 PIECE = 256
 EPSILON = 1e-05
 NEGATIVE = -1e30
+
+
+def collect(array, axis, dim):
+    ways, here, hop = (lax.axis_size(axis), lax.axis_index(axis), array.shape[dim])
+    dims = [n * ways if d == dim else n for d, n in enumerate(array.shape)]
+    full = lax.dynamic_update_slice_in_dim(
+        jnp.zeros(dims, array.dtype), array, here * hop, axis=dim
+    )
+    going_up = going_down = array
+    for far in range(1, ways // 2 + 1):
+        going_up = lax.ppermute(going_up, axis, [(d, (d + 1) % ways) for d in range(ways)])
+        full = lax.dynamic_update_slice_in_dim(full, going_up, (here - far) % ways * hop, axis=dim)
+        if 2 * far < ways:
+            going_down = lax.ppermute(going_down, axis, [(d, (d - 1) % ways) for d in range(ways)])
+            full = lax.dynamic_update_slice_in_dim(
+                full, going_down, (here + far) % ways * hop, axis=dim
+            )
+    return full
 
 
 def layer_norm(values, gain, shift):
@@ -181,7 +199,7 @@
         lax.all_gather(w_query, "dp", axis=0, tiled=True),
         lax.all_gather(w_key, "dp", axis=0, tiled=True),
         lax.all_gather(w_value, "dp", axis=0, tiled=True),
-        lax.all_gather(w_output, "dp", axis=1, tiled=True),
+        collect(w_output, "dp", 1),
     )
     inner_w, outer_w = (
         lax.all_gather(w_in, "dp", axis=0, tiled=True),

time: 1110 us -> 1090 us (0.982)
  blocking collectives: 173 us -> 139 us
  starting transfers between devices: 1.07 us -> 16.4 us
    all_gather x1 -> x0, blocking collectives: 34.9 us -> none  [per_device(): lax.all_gather(w_output, 'dp', axis=1, tiled=True)]
    ppermute x0 -> x7, starting transfers between devices: none -> 14.7 us  [the longest x3 14.7 us: collect(): lax.ppermute(going_down, axis, [(d, (d - 1) % ways) for d in range(ways)])]
  transfers between devices with their start and end apart: 16 -> 23, of which waited for: 14 -> 15; matrix products, arithmetic and copies ran while one was open for 8% -> 8% of each run, Pallas kernels for 0% -> 0%
where the time goes in v1:
time: 1090 us; the launch traced here: 1080 us
  waiting for transfers between devices  657 us (60%)
  blocking collectives  139 us (13%)
  matrix products  130 us (12%)
  other arithmetic  67.8 us (6%)
  local copies, waits for them, and re-layouts  56.9 us (5%)
  between operations  16.7 us (2%)
  starting transfers between devices  16.4 us (2%)
    reduce_scatter x2, waiting for transfers between devices, merge_rows(): lax.psum_scatter(jnp.dot(source, weight, preferred_element_type=jnp.float...  120 us
    reduce_scatter x2, waiting for transfers between devices, return_rows(): return lax.psum_scatter(running, 'tensor', scatter_dimension=0, tiled=True)  109 us
    reduce_scatter x1, waiting for transfers between devices, per_device(): lax.psum_scatter(grad_outer, 'dp', scatter_dimension=1, tiled=True)  72.6 us
    reduce_scatter x1, waiting for transfers between devices, per_device(): lax.psum_scatter(grad_value_w, 'dp', scatter_dimension=0, tiled=True)  65.7 us
    reduce_scatter x1, waiting for transfers between devices, per_device(): lax.psum_scatter(grad_query_w, 'dp', scatter_dimension=0, tiled=True)  65.7 us
    reduce_scatter x1, waiting for transfers between devices, per_device(): lax.psum_scatter(grad_key_w, 'dp', scatter_dimension=0, tiled=True)  65.5 us
    all_gather x2, waiting for transfers between devices, share_grad(): return lax.all_gather(local_rows, 'tensor', axis=0, tiled=True)  57.3 us
    psum x1, blocking collectives, per_device(): lax.psum((layer_one[1], layer_one[2], layer_two[1], layer_two[2], bias_fu...  40.8 us
  transfers between devices with their start and end apart: 23, of which 15 were waited for; matrix products, arithmetic and copies ran while one was open for 8% of the time, Pallas kernels for 0%

profile of v1, /device:TPU:0, one launch (start us, length us, event | category | flops | bytes accessed | tf_op | source)
XLA Modules:
  0.0 1084.3 jit_solution(3797597194403206540)
XLA Ops:
  13.1 6.0 collective-permute-start.1
  19.5 2.9 and_reduce_fusion
  25.9 32.2 %all_gather.29 = bf16[768,192]{1,0:T(8,128)(2,1)S(1)} all-gather(bf16[96,192]{1,0:T(8,128)(2,1)S(1)} %copy-done.46), channel_id=1, replica_groups=mesh['dp'=8,'tensor'=4] {'dp'}, dimensions={0}, use_global_device_ids=true | all-gather | bytes 331776 | tf_op jit(solution)/shard_map/all_gather | solution.py:199
  58.1 3.9 collective-permute-start.3
  62.0 33.0 %all_gather.30 = bf16[768,192]{1,0:T(8,128)(2,1)} all-gather(bf16[96,192]{1,0:T(8,128)(2,1)S(1)} %copy-done.47), channel_id=1, replica_groups=mesh['dp'=8,'tensor'=4] {'dp'}, dimensions={0}, use_global_device_ids=true | all-gather | bytes 331776 | tf_op jit(solution)/shard_map/all_gather | solution.py:200
  95.0 4.8 collective-permute-start.5
  99.8 33.4 %all_gather.28 = bf16[768,192]{1,0:T(8,128)(2,1)} all-gather(bf16[96,192]{1,0:T(8,128)(2,1)S(1)} %copy-done.48), channel_id=1, replica_groups=mesh['dp'=8,'tensor'=4] {'dp'}, dimensions={0}, use_global_device_ids=true | all-gather | bytes 331776 | tf_op jit(solution)/shard_map/all_gather | solution.py:201
  133.2 4.4 copy.83
  142.2 4.2 convolution_convert_fusion.1
  146.3 3.2 convert_element_type.101
  149.6 2.2 copy.82
  151.8 3.3 fusion.107
  155.1 3.4 reshape.244
  158.5 3.2 fusion.103
  161.7 2.3 fusion.106
  164.0 2.8 reshape.243
  171.7 27.8 %while.26 = (s32[]{:T(128)}, bf16[2,1024,3,64]{1,3,2,0:T(8,128)(2,1)}, f32[2,3,1024,1]{2,1,3,0:T(4,128)S(1)}, bf16[2,1024,3,64]{1,3,2,0:T(8,128)(2,1)}, pred[2,1...) while((s32[]{:T(128)}, ...), condition=%wide.region_6.7_spmd, body=%wide.region_3.6_spmd.sunk | while | flops 843248640 | bytes 55163064 | solution.py:104
  173.3 2.6 fusion.174
  175.9 3.9 fusion.175
  179.8 5.7 fusion.176
  187.2 2.6 fusion.174
  189.8 3.9 fusion.175
  193.7 5.7 fusion.176
  202.5 3.7 fusion.108
  207.0 59.3 %reduce-scatter.13.cloned.1.call-done = f32[512,768]{1,0:T(8,128)} async-done(((f32[2048,768]{1,0:T(8,128)}), f32[512,768]{1,0:T(8,128)}) %reduce-scatter.13.cloned.1.call-update) | async-done | bytes 1572880 | tf_op jit(solution)/shard_map/reduce_scatter | solution.py:185
  273.6 24.4 %all-gather.9.cloned.1.call-done = bf16[2048,768]{1,0:T(8,128)(2,1)} async-done(((bf16[512,768]{1,0:T(8,128)(2,1)}), bf16[2048,768]{1,0:T(8,128)(2,1)}) %all-gather.9.cloned.1.call-update) | async-done | bytes 3145744 | tf_op jit(solution)/shard_map/all_gather | solution.py:179
  298.0 7.5 fusion.109
  305.5 36.3 %all-gather.13.cloned.1.call-done = bf16[768,768]{0,1:T(8,128)(2,1)} async-done(((bf16[768,96]{0,1:T(8,128)(2,1)}), bf16[768,768]{0,1:T(8,128)(2,1)}) %all-gather.13.cloned.1.call-update) | async-done | bytes 1179664 | tf_op jit(solution)/shard_map/all_gather | solution.py:206
  341.8 29.1 %all-gather.15.cloned.1.call-done = bf16[2048,768]{1,0:T(8,128)(2,1)} async-done(((bf16[512,768]{1,0:T(8,128)(2,1)}), bf16[2048,768]{1,0:T(8,128)(2,1)}) %all-gather.15.cloned.1.call-update) | async-done | bytes 3145744 | tf_op jit(solution)/shard_map/all_gather | solution.py:182
  370.9 10.9 %convert_reduce_fusion = (f32[768]{0:T(1024)}, bf16[2048,768]{1,0:T(8,128)(2,1)S(1)}, bf16[2048,768]{1,0:T(8,128)(2,1)}) fusion(f32[2048,768]{1,0:T(8,128)} %fusion.109, f32[768]{0:T(1024)S(1)} %dynamic_slice.36, bf16[2048,768]{1,0:T(8,128)(2,1)} %all-gather.15.cloned.1.call-done, bf16[768,768]{0,1:T(8,128)(2,1)} %all-gather.13.cloned.1.call-done), kind=kOutput, calls=%fused_computation.73 | convolution fusion | flops 2455239936 | bytes 16914432 | tf_op jit(solution)/shard_map/dot_general | solution.py:75
  383.5 4.5 fusion.111
  388.1 8.0 fusion.110
  396.2 50.2 %reduce-scatter.17.cloned.1.call-done = f32[512,768]{1,0:T(8,128)} async-done(((f32[2048,768]{1,0:T(8,128)}), f32[512,768]{1,0:T(8,128)}) %reduce-scatter.17.cloned.1.call-update) | async-done | bytes 1572880 | tf_op jit(solution)/shard_map/reduce_scatter | solution.py:196
  446.4 60.8 %reduce-scatter.15.cloned.1.call-done = f32[512,768]{1,0:T(8,128)} async-done(((f32[2048,768]{1,0:T(8,128)}), f32[512,768]{1,0:T(8,128)}) %reduce-scatter.15.cloned.1.call-update) | async-done | bytes 1572880 | tf_op jit(solution)/shard_map/reduce_scatter | solution.py:185
  507.2 8.4 multiply_reduce_fusion.1
  519.8 28.2 %all-gather.17.cloned.1.call-done = bf16[2048,768]{1,0:T(8,128)(2,1)} async-done(((bf16[512,768]{1,0:T(8,128)(2,1)}), bf16[2048,768]{1,0:T(8,128)(2,1)}) %all-gather.17.cloned.1.call-update) | async-done | bytes 3145744 | tf_op jit(solution)/shard_map/all_gather | solution.py:182
  548.0 3.1 convolution_convert_fusion
  554.9 51.3 %while.27 = (s32[]{:T(128)}, f32[2,1024,3,64]{1,3,2,0:T(8,128)}, f32[2,1024,3,64]{1,3,2,0:T(8,128)}, bf16[2,1024,3,64]{1,3,2,0:T(8,128)(2,1)}, bf16[2,1024,3,64]...) while((s32[]{:T(128)}, f32[2,1024,3,64]{1,3,2,0:T(8,128)}, ...), condition=%wide.region_16.17_spmd, body=%wide.region_14.16_spmd.sunk | while | flops 2061038592 | bytes 135890256 | solution.py:138
  558.1 3.7 fusion.188
  561.8 7.2 multiply_reduce_fusion.5
  569.0 7.1 multiply_convert_fusion.3
  576.1 2.0 fusion.187
  583.7 3.7 fusion.188
  587.4 7.2 multiply_reduce_fusion.5
  594.6 7.1 multiply_convert_fusion.3
  601.7 2.0 fusion.187
  606.2 4.5 convolution_bitcast_fusion
  618.2 3.8 add_add_fusion
  623.9 6.0 fusion.117
  630.2 7.1 fusion.118
  637.4 3.1 fusion.116
  640.5 3.0 fusion.115
  644.0 4.1 fusion.114
  648.1 25.2 %reduce-scatter.31.cloned.1.call-done = f32[96,192]{1,0:T(8,128)} async-done(((f32[768,192]{1,0:T(8,128)}), f32[96,192]{1,0:T(8,128)}) %reduce-scatter.31.cloned.1.call-update) | async-done | bytes 73744
  674.9 58.7 %reduce-scatter.19.cloned.1.call-done = f32[512,768]{1,0:T(8,128)} async-done(((f32[2048,768]{1,0:T(8,128)}), f32[512,768]{1,0:T(8,128)}) %reduce-scatter.19.cloned.1.call-update) | async-done | bytes 1572880 | tf_op jit(solution)/shard_map/reduce_scatter | solution.py:196
  736.5 9.1 fusion.90
  745.6 3.3 stack.43
  748.9 40.8 %all-reduce = (f32[768]{0:T(1024)}, f32[768]{0:T(1024)}, f32[768]{0:T(1024)}, f32[768]{0:T(1024)}, f32[3072]{0:T(1024)}, /*index=5*/f32[768]{0:T(1024)}, f32[5]{0:T(128)}) all-reduce(f32[768]{0:T(1024)S(1)} %get-tuple-element.187, f32[768]{0:T(1024)S(1)} %get-tuple-element.191, ...), channel_id=1, replica_groups=mesh['dp'=8,'tensor'=4] {'dp','tensor'}, use_global_device_ids=true, to_apply=%region_27.28 | all-reduce | flops 6917 | bytes 55336 | tf_op jit(solution)/shard_map/psum | solution.py:280
  789.7 4.6 pad_maximum_fusion
  794.3 12.9 %reduce-scatter.27.cloned.1.call-done = f32[96,768]{1,0:T(8,128)} async-done(((f32[768,768]{1,0:T(8,128)}), f32[96,768]{1,0:T(8,128)}) %reduce-scatter.27.cloned.1.call-update) | async-done | bytes 294928 | tf_op jit(solution)/shard_map/reduce_scatter | solution.py:277
  807.2 72.6 %reduce-scatter.29.cloned.1.call-done = f32[768,96]{0,1:T(8,128)} async-done(((f32[768,768]{0,1:T(8,128)}), f32[768,96]{0,1:T(8,128)}) %reduce-scatter.29.cloned.1.call-update) | async-done | bytes 294928 | tf_op jit(solution)/shard_map/reduce_scatter | solution.py:278
  879.8 65.7 %reduce-scatter.25.cloned.1.call-done = f32[96,192]{1,0:T(8,128)} async-done(((f32[768,192]{1,0:T(8,128)}), f32[96,192]{1,0:T(8,128)}) %reduce-scatter.25.cloned.1.call-update) | async-done | bytes 73744 | tf_op jit(solution)/shard_map/reduce_scatter | solution.py:275
  945.6 65.5 %reduce-scatter.23.cloned.1.call-done = f32[96,192]{1,0:T(8,128)} async-done(((f32[768,192]{1,0:T(8,128)}), f32[96,192]{1,0:T(8,128)}) %reduce-scatter.23.cloned.1.call-update) | async-done | bytes 73744 | tf_op jit(solution)/shard_map/reduce_scatter | solution.py:274
  1011.1 65.7 %reduce-scatter.21.cloned.1.call-done = f32[96,192]{1,0:T(8,128)} async-done(((f32[768,192]{1,0:T(8,128)}), f32[96,192]{1,0:T(8,128)}) %reduce-scatter.21.cloned.1.call-update) | async-done | bytes 73744 | tf_op jit(solution)/shard_map/reduce_scatter | solution.py:273
  (271 shorter events, 67.5 us)
Async XLA Ops:
  8.0 3.0 copy-start.1
  8.0 5.0 copy-start.49
  8.0 134.2 %all-gather.7.cloned.1.call-start = ((), (), s32[]{:S(2)}) async-start(), calls=%async_computation.10 | async-start | bytes 3932160 | tf_op jit(solution)/shard_map/all_gather | solution.py:179
  9.5 9.9 copy-start.62
  11.0 8.5 copy-start.55
  11.0 8.5 copy-start.51
  13.0 253.3 %reduce-scatter.13.cloned.1.call-start = ((), (), s32[]{:S(2)}) async-start(), calls=%async_computation.11 | async-start | bytes 7864320 | tf_op jit(solution)/shard_map/reduce_scatter | solution.py:185
  13.1 45.0 %collective-permute-start.1 = (bf16[192,96]{1,0:T(8,128)(2,1)S(1)}, bf16[192,96]{1,0:T(8,128)(2,1)S(1)}, u32[]{:S(2)}, u32[]{:S(2)}) collective-permute-start(bf16[192,96]{1,0:T(8,128)(2,1)S(1)} %copy-done.49), channel_id=1, source_target_pairs={{0,28},{4,0},{8,4},{12,8},{16,12},{20,16},{24,20},{28,24},{1,29},{... | collective-permute-start | bytes 110600 | tf_op jit(solution)/shard_map/ppermute | solution.py:24
  19.1 6.8 collective-permute-start
  22.4 3.5 copy-start.46
  22.4 39.5 %copy-start.47 = (bf16[96,192]{1,0:T(8,128)(2,1)S(1)}, bf16[96,192]{1,0:T(8,128)(2,1)}, u32[]{:S(2)}) copy-start(bf16[96,192]{1,0:T(8,128)(2,1)} %param.26) | copy-start | bytes 110596
  22.5 77.3 %copy-start.48 = (bf16[96,192]{1,0:T(8,128)(2,1)S(1)}, bf16[96,192]{1,0:T(8,128)(2,1)}, u32[]{:S(2)}) copy-start(bf16[96,192]{1,0:T(8,128)(2,1)} %param.27) | copy-start | bytes 110596
  25.9 36.1 %collective-permute-start.2 = (bf16[192,96]{1,0:T(8,128)(2,1)S(1)}, bf16[192,96]{1,0:T(8,128)(2,1)S(1)}, u32[]{:S(2)}, u32[]{:S(2)}) collective-permute-start(bf16[192,96]{1,0:T(8,128)(2,1)S(1)} %collective-permute-done), channel_id=1, source_target_pairs={{0,4},{4,8},{8,12},{12,16},{16,20},{20,24},{24,28},{28,0},{1,5},{5... | collective-permute-start | bytes 110600 | tf_op jit(solution)/shard_map/ppermute | solution.py:21
  58.1 103.6 %copy-start.20 = (bf16[768,192]{1,0:T(8,128)(2,1)}, bf16[768,192]{1,0:T(8,128)(2,1)S(1)}, u32[]{:S(2)}) copy-start(bf16[768,192]{1,0:T(8,128)(2,1)S(1)} %all_gather.29) | copy-start | bytes 884740
  58.1 36.9 %collective-permute-start.3 = (bf16[192,96]{1,0:T(8,128)(2,1)S(1)}, bf16[192,96]{1,0:T(8,128)(2,1)S(1)}, u32[]{:S(2)}, u32[]{:S(2)}) collective-permute-start(bf16[192,96]{1,0:T(8,128)(2,1)S(1)} %collective-permute-done.1), channel_id=1, source_target_pairs={{0,28},{4,0},{8,4},{12,8},{16,12},{20,16},{24,20},{28,24},{1,29},{... | collective-permute-start | bytes 110600 | tf_op jit(solution)/shard_map/ppermute | solution.py:24
  62.0 37.8 %collective-permute-start.4 = (bf16[192,96]{1,0:T(8,128)(2,1)S(1)}, bf16[192,96]{1,0:T(8,128)(2,1)S(1)}, u32[]{:S(2)}, u32[]{:S(2)}) collective-permute-start(bf16[192,96]{1,0:T(8,128)(2,1)S(1)} %collective-permute-done.2), channel_id=1, source_target_pairs={{0,4},{4,8},{8,12},{12,16},{16,20},{20,24},{24,28},{28,0},{1,5},{5... | collective-permute-start | bytes 110600 | tf_op jit(solution)/shard_map/ppermute | solution.py:21
  95.0 45.6 %collective-permute-start.5 = (bf16[192,96]{1,0:T(8,128)(2,1)S(1)}, bf16[192,96]{1,0:T(8,128)(2,1)S(1)}, u32[]{:S(2)}, u32[]{:S(2)}) collective-permute-start(bf16[192,96]{1,0:T(8,128)(2,1)S(1)} %collective-permute-done.3), channel_id=1, source_target_pairs={{0,28},{4,0},{8,4},{12,8},{16,12},{20,16},{24,20},{28,24},{1,29},{... | collective-permute-start | bytes 110600 | tf_op jit(solution)/shard_map/ppermute | solution.py:24
  99.8 41.4 %collective-permute-start.6 = (bf16[192,96]{1,0:T(8,128)(2,1)S(1)}, bf16[192,96]{1,0:T(8,128)(2,1)S(1)}, u32[]{:S(2)}, u32[]{:S(2)}) collective-permute-start(bf16[192,96]{1,0:T(8,128)(2,1)S(1)} %collective-permute-done.4), channel_id=1, source_target_pairs={{0,4},{4,8},{8,12},{12,16},{16,20},{20,24},{24,28},{28,0},{1,5},{5... | collective-permute-start | bytes 110600 | tf_op jit(solution)/shard_map/ppermute | solution.py:21
  142.2 9.6 copy-start.8
  199.4 3.1 copy-start.37
  206.3 60.0 %copy-start.2 = (bf16[512,768]{1,0:T(8,128)(2,1)S(1)}, bf16[512,768]{1,0:T(8,128)(2,1)}, u32[]{:S(2)}) copy-start(bf16[512,768]{1,0:T(8,128)(2,1)} %param.21) | copy-start | bytes 2359300
  206.3 67.2 %all-gather.11.cloned.1.call-start = ((), (), s32[]{:S(2)}) async-start(), calls=%async_computation.13 | async-start | bytes 1327104 | tf_op jit(solution)/shard_map/all_gather | solution.py:205
  206.9 61.4 %copy-start.50 = (f32[768]{0:T(1024)S(1)}, f32[768]{0:T(1024)}, u32[]{:S(2)}) copy-start(f32[768]{0:T(1024)} %param.33) | copy-start | bytes 9220
  206.9 61.4 %copy-start.60 = (f32[768]{0:T(1024)S(1)}, f32[768]{0:T(1024)}, u32[]{:S(2)}) copy-start(f32[768]{0:T(1024)} %param.34) | copy-start | bytes 9220
  206.9 91.1 %all-gather.9.cloned.1.call-start = ((), (), s32[]{:S(2)}) async-start(), calls=%async_computation.12 | async-start | bytes 3932160 | tf_op jit(solution)/shard_map/all_gather | solution.py:179
  267.9 3.1 copy-start.13
  269.5 72.3 %all-gather.13.cloned.1.call-start = ((), (), s32[]{:S(2)}) async-start(), calls=%async_computation.14 | async-start | bytes 1327104 | tf_op jit(solution)/shard_map/all_gather | solution.py:206
  270.1 100.9 %all-gather.15.cloned.1.call-start = ((), (), s32[]{:S(2)}) async-start(), calls=%async_computation.16 | async-start | bytes 3932160 | tf_op jit(solution)/shard_map/all_gather | solution.py:182
  272.7 173.7 %reduce-scatter.17.cloned.1.call-start = ((), (), s32[]{:S(2)}) async-start(), calls=%async_computation.17 | async-start | bytes 7864320 | tf_op jit(solution)/shard_map/reduce_scatter | solution.py:196
  370.9 12.6 %copy-start.65 = (bf16[768,768]{1,0:T(8,128)(2,1)S(1)}, bf16[768,768]{1,0:T(8,128)(2,1)}, u32[]{:S(2)}) copy-start(bf16[768,768]{1,0:T(8,128)(2,1)} %all-gather.11.cloned.1.call-done) | copy-start | bytes 3538948
  388.1 119.2 %reduce-scatter.15.cloned.1.call-start = ((), (), s32[]{:S(2)}) async-start(), calls=%async_computation.15 | async-start | bytes 7864320 | tf_op jit(solution)/shard_map/reduce_scatter | solution.py:185
  396.1 111.1 %copy-start.61 = (f32[768]{0:T(1024)S(1)}, f32[768]{0:T(1024)}, u32[]{:S(2)}) copy-start(f32[768]{0:T(1024)} %param.36) | copy-start | bytes 9220
  396.1 151.9 %all-gather.17.cloned.1.call-start = ((), (), s32[]{:S(2)}) async-start(), calls=%async_computation.18 | async-start | bytes 3932160 | tf_op jit(solution)/shard_map/all_gather | solution.py:182
  507.2 8.4 copy-start.16
  516.3 3.5 copy-start.53
  519.3 153.9 %reduce-scatter.31.cloned.1.call-start = ((), (), s32[]{:S(2)}) async-start(), calls=%async_computation.25 | async-start | bytes 884736
  551.1 3.8 copy-start.5
  551.1 3.8 copy-start.7
  551.1 3.8 copy-start.15
  561.8 7.2 copy-start.28
  569.0 7.1 copy-start.30
  587.4 7.2 copy-start.28
  594.6 7.1 copy-start.30
  606.1 4.8 copy-start.32
  606.1 4.8 copy-start.35
  606.1 4.8 copy-start.39
  606.2 4.8 copy-start.40
  610.7 122.9 %reduce-scatter.19.cloned.1.call-start = ((), (), s32[]{:S(2)}) async-start(), calls=%async_computation.19 | async-start | bytes 7864320 | tf_op jit(solution)/shard_map/reduce_scatter | solution.py:196
  622.0 185.2 %reduce-scatter.27.cloned.1.call-start = ((), (), s32[]{:S(2)}) async-start(), calls=%async_computation.23 | async-start | bytes 2654208 | tf_op jit(solution)/shard_map/reduce_scatter | solution.py:277
  629.9 249.9 %reduce-scatter.29.cloned.1.call-start = ((), (), s32[]{:S(2)}) async-start(), calls=%async_computation.24 | async-start | bytes 2654208 | tf_op jit(solution)/shard_map/reduce_scatter | solution.py:278
  630.2 7.2 copy-start.9
  637.3 308.3 %reduce-scatter.25.cloned.1.call-start = ((), (), s32[]{:S(2)}) async-start(), calls=%async_computation.22 | async-start | bytes 884736 | tf_op jit(solution)/shard_map/reduce_scatter | solution.py:275
  640.5 3.2 copy-start.63
  640.5 370.6 %reduce-scatter.23.cloned.1.call-start = ((), (), s32[]{:S(2)}) async-start(), calls=%async_computation.21 | async-start | bytes 884736 | tf_op jit(solution)/shard_map/reduce_scatter | solution.py:274
  643.6 433.1 %reduce-scatter.21.cloned.1.call-start = ((), (), s32[]{:S(2)}) async-start(), calls=%async_computation.20 | async-start | bytes 884736 | tf_op jit(solution)/shard_map/reduce_scatter | solution.py:273
  644.0 89.6 %copy-start.3 = (bf16[512,768]{1,0:T(8,128)(2,1)S(1)}, bf16[512,768]{1,0:T(8,128)(2,1)}, u32[]{:S(2)}) copy-start(bf16[512,768]{1,0:T(8,128)(2,1)} %param.21) | copy-start | bytes 2359300
  644.0 89.6 %copy-start.44 = (f32[512]{0:T(512)S(1)}, f32[512]{0:T(512)}, u32[]{:S(2)}) copy-start(f32[512]{0:T(512)} %copy-done.43) | copy-start | bytes 6148
  644.0 89.6 %copy-start.45 = (f32[768]{0:T(1024)S(1)}, f32[768]{0:T(1024)}, u32[]{:S(2)}) copy-start(f32[768]{0:T(1024)} %param.31) | copy-start | bytes 9220
  648.0 87.6 %copy-start.56 = (f32[512]{0:T(512)S(1)}, f32[512]{0:T(512)}, u32[]{:S(2)}) copy-start(f32[512]{0:T(512)} %copy-done.55) | copy-start | bytes 6148
  648.0 87.6 %copy-start.52 = (f32[512]{0:T(512)S(1)}, f32[512]{0:T(512)}, u32[]{:S(2)}) copy-start(f32[512]{0:T(512)} %copy-done.51) | copy-start | bytes 6148
  674.9 61.5 %copy-start.14 = (bf16[512,768]{1,0:T(8,128)(2,1)S(1)}, bf16[512,768]{1,0:T(8,128)(2,1)}, u32[]{:S(2)}) copy-start(bf16[512,768]{1,0:T(8,128)(2,1)} %param.23) | copy-start | bytes 2359300
  674.9 61.5 %copy-start.54 = (f32[512]{0:T(512)S(1)}, f32[512]{0:T(512)}, u32[]{:S(2)}) copy-start(f32[512]{0:T(512)} %copy-done.53) | copy-start | bytes 6148
  736.5 12.4 %copy-start.57 = (f32[768]{0:T(1024)S(1)}, f32[768]{0:T(1024)}, u32[]{:S(2)}) copy-start(f32[768]{0:T(1024)} %get-tuple-element.185) | copy-start | bytes 9220
  736.5 12.4 %copy-start.58 = (f32[768]{0:T(1024)S(1)}, f32[768]{0:T(1024)}, u32[]{:S(2)}) copy-start(f32[768]{0:T(1024)} %get-tuple-element.190) | copy-start | bytes 9220
  (35 other events, 56.0 us)
Sparse Core Ops, SparseCore 0:
  13.1 31.2 all-gather.6
  206.4 59.8 reduce-scatter.12
  519.5 28.5 all-gather.16
Sparse Core Ops, SparseCore 1:
  209.0 42.9 all-gather.10
  269.6 28.3 all-gather.8
  300.3 41.5 all-gather.12
  344.0 26.8 all-gather.14
  388.1 58.2 reduce-scatter.16
  449.0 58.2 reduce-scatter.14
  610.8 62.4 reduce-scatter.30
  676.3 57.3 reduce-scatter.18
  737.9 69.3 reduce-scatter.26
  811.7 68.0 reduce-scatter.28
  883.9 61.6 reduce-scatter.24
  949.5 61.6 reduce-scatter.22
  1015.2 61.5 reduce-scatter.20
